TPU v7x, 512 devices: a whole 4x8x8 slice. The times are simulated.
512 devices in a mesh: leaf: 128 (over z, y, core), sep: 4 (over x).
Axes of the slice: x: 4, y: 8, z: 8, core: 2. Of those that a mesh axis runs over, the one named last changes fastest.
Arguments:
- leaf_source: float32 [128, 640, 256], P('leaf', 'sep'), may hold values from -6 to 6
- leaf_inverse: float32 [128, 640, 640], P('leaf', 'sep'), as said below
- leaf_update: float32 [128, 896, 640], P('leaf', None, 'sep'), as said below
- row_lists: int32 [128, 896], P('leaf'), may hold values from 0 to 255
- row_counts: int32 [128, 7], P('leaf'), may hold values from 1 to 128, as said below
- separator_source: float32 [128, 256, 256], P('leaf', 'sep'), may hold values from -6 to 6
- separator_inverse: float32 [128, 256, 256], P('leaf'), as said below
- separator_coupling: float32 [128, 256, 256], P('leaf'), may hold values from -0.1875 to 0.1875
Outputs:
- leaf_solution: float32 [128, 640, 256], P('leaf', 'sep')
- separator_solution: float32 [128, 256, 256], P('leaf', 'sep')
Inputs may be any that keep to these rules, and one draw needn't show every extreme that they name: `leaf_inverse`: each leaf's block is lower triangular, zero above the diagonal, with diagonal entries between 0.6 and 1.4. `separator_inverse`: each block is lower triangular, zero above the diagonal, with diagonal entries between 0.6 and 1.4. `leaf_update`: row r of a leaf's block belongs to the leaf's ancestor of level 1 + r // 128. `row_lists`: entry r names a row of the leaf's ancestor of level 1 + r // 128. `row_counts`: at every level some leaf has 128 live rows.
All inputs are finite; a program needn't handle non-finite values.
Results may differ from a plain program's by a relative error of at most 0.00011.
Values sent between devices are 32-bit elements; how exact they have to be, the bound alone decides.
A program may use at most 64 MiB of HBM per device.

v0:
```python
import jax
import jax.numpy as jnp
from jax import lax
from jax.sharding import PartitionSpec as P

highest = lax.Precision.HIGHEST


def passed_along(x, axis, by):
    peers = lax.axis_size(axis)
    pairs = [(i, i + by) for i in range(peers) if 0 <= i + by < peers]
    return lax.ppermute(x, axis, pairs)


def product(matrix, operand):
    return jnp.dot(matrix, operand, precision=highest, preferred_element_type=jnp.float32)


def product_first(matrix, operand):
    return lax.dot_general(
        matrix,
        operand,
        (((0,), (0,)), ((), ())),
        precision=highest,
        preferred_element_type=jnp.float32,
    )


def tree_pass(payload, offset):
    return passed_along(payload, "leaf", offset)


def sep_rows(payload):
    return lax.all_gather(payload, "sep", axis=0, tiled=True)


def per_device(
    leaf_source,
    leaf_inverse,
    leaf_update,
    row_lists,
    row_counts,
    separator_source,
    separator_inverse,
    separator_coupling,
):
    depth = row_counts.shape[1]
    leaf_index = lax.axis_index("leaf")
    sep_index = lax.axis_index("sep")
    source = leaf_source[0]
    inverse = leaf_inverse[0]
    update = leaf_update[0]
    quarter = separator_source.shape[1]
    full_rows = separator_inverse.shape[1]
    columns = source.shape[1]
    capacity = row_lists.shape[1] // depth
    first_row = sep_index * quarter
    inverse_block = inverse
    leaf_y = product(inverse_block, lax.all_gather(source, "sep", axis=0, tiled=True))
    slot_index = jnp.arange(depth * capacity) % capacity
    limits = jnp.repeat(row_counts[0], capacity)
    live_rows = (slot_index < limits)[:, None]
    update_terms = jnp.where(live_rows, product(update, leaf_y), 0.0)
    targets = row_lists[0].reshape(depth, capacity)
    picker = (jnp.arange(full_rows)[None, :, None] == targets[:, None, :]).astype(jnp.float32)
    densified = jnp.einsum(
        "kwp,kpn->wkn",
        picker,
        update_terms.reshape(depth, capacity, columns),
        precision=highest,
        preferred_element_type=jnp.float32,
    )
    carried = lax.psum_scatter(densified, "sep", scatter_dimension=0, tiled=True)
    own_source = separator_source[0]
    solver_block = separator_inverse[0]
    coupling = separator_coupling[0]
    coupling_rows = lax.dynamic_slice_in_dim(coupling, first_row, quarter, 0)
    solved_down = jnp.zeros((full_rows, columns), jnp.float32)
    for height in range(1, depth + 1):
        upper_slots = carried[:, height - 1 :]
        stride = 2 ** max(height - 2, 0)
        from_left = tree_pass(upper_slots, stride)
        if height == 1:
            from_right = upper_slots
        else:
            from_right = tree_pass(upper_slots, -stride)
        is_owner = leaf_index % 2**height == 2 ** (height - 1)
        carried = carried.at[:, height - 1 :].set(
            jnp.where(is_owner, from_left + from_right, upper_slots)
        )
        residual_full = sep_rows(own_source - carried[:, height - 1])
        solved = product(solver_block, residual_full)
        solved_down = jnp.where(is_owner, solved, solved_down)
        if height < depth:
            carried = carried.at[:, height].add(
                jnp.where(is_owner, product(coupling_rows, solved), 0.0)
            )
    stacked = jnp.zeros(carried.shape, jnp.float32)
    solution_full = jnp.zeros((full_rows, columns), jnp.float32)
    for height in range(depth, 0, -1):
        is_owner = leaf_index % 2**height == 2 ** (height - 1)
        target = solved_down
        if height < depth:
            stride = 2 ** (height - 1)
            upper_slots = stacked[:, height:]
            from_below = tree_pass(upper_slots, stride)
            from_above = tree_pass(upper_slots, -stride)
            right_child = leaf_index // 2**height % 2 == 1
            received = jnp.where(right_child, from_below, from_above)
            stacked = stacked.at[:, height:].set(jnp.where(is_owner, received, upper_slots))
            parent_full = sep_rows(received[:, 0])
            target = solved_down - product_first(coupling, parent_full)
        solution = product_first(solver_block, target)
        solution_full = jnp.where(is_owner, solution, solution_full)
        own_rows = lax.dynamic_slice_in_dim(solution, first_row, quarter, 0)
        stacked = stacked.at[:, height - 1].set(
            jnp.where(is_owner, own_rows, stacked[:, height - 1])
        )
    from_next = tree_pass(stacked, -1)
    ancestors = jnp.where(leaf_index % 2 == 1, stacked, from_next)
    ancestors_full = sep_rows(ancestors)
    picked = jnp.einsum(
        "kwp,wkn->kpn",
        picker,
        ancestors_full,
        precision=highest,
        preferred_element_type=jnp.float32,
    )
    picked = jnp.where(live_rows, picked.reshape(depth * capacity, columns), 0.0)
    leaf_w = leaf_y - product_first(update, picked)
    inverse_block = inverse
    leaf_x = lax.psum_scatter(
        product_first(inverse_block, leaf_w), "sep", scatter_dimension=0, tiled=True
    )
    separator_rows = lax.dynamic_slice_in_dim(solution_full, first_row, quarter, 0)
    return (leaf_x[None], separator_rows[None])


def solution(mesh):
    placed = (
        P("leaf", "sep", None),
        P("leaf", "sep", None),
        P("leaf", None, "sep"),
        P("leaf", None),
        P("leaf", None),
        P("leaf", "sep", None),
        P("leaf", None, None),
        P("leaf", None, None),
    )
    return jax.shard_map(
        per_device,
        mesh=mesh,
        in_specs=placed,
        out_specs=(P("leaf", "sep", None), P("leaf", "sep", None)),
        check_vma=False,
    )
```

profile of v0, /device:TPU:8, one launch (start us, length us, event | category | flops | bytes accessed | tf_op | source)
XLA Modules:
  0.0 518.3 jit_solution(3606953752508697259)
XLA Ops:
  7.2 13.7 %all-gather = f32[1,640,256]{2,1,0:T(8,128)S(1)} all-gather(f32[1,160,256]{2,1,0:T(8,128)} %param.62), channel_id=2, replica_groups=mesh['leaf'=128,'sep'=4] {'sep'}, dimensions={1}, use_global_device_ids=true | all-gather | bytes 819200 | tf_op jit(solution)/shard_map/all_gather | solution.py:59
  27.9 39.7 %reduce-scatter.5.cloned.1.call-done = f32[64,7,256]{2,1,0:T(8,128)} async-done(((f32[256,7,256]{2,1,0:T(8,128)}), f32[64,7,256]{2,1,0:T(8,128)}) %reduce-scatter.5.cloned.1.call-update) | async-done | bytes 458768 | tf_op jit(solution)/shard_map/reduce_scatter | solution.py:73
  70.7 7.9 %collective-permute-done = f32[64,7,256]{2,0,1:T(8,128)S(1)} collective-permute-done((f32[64,7,256]{2,0,1:T(8,128)S(1)}, f32[64,7,256]{2,0,1:T(8,128)S(1)}, u32[]{:S(2)}, u32[]{:S(2)}) %collective-permute-start) | collective-permute-done | bytes 458784 | tf_op jit(solution)/shard_map/ppermute | solution.py:12
  79.8 12.4 %all_gather.46 = f32[256,256]{1,0:T(8,128)S(1)} all-gather(f32[64,256]{1,0:T(8,128)S(1)} %fusion.94), channel_id=1, replica_groups=mesh['leaf'=128,'sep'=4] {'sep'}, dimensions={0}, use_global_device_ids=true | all-gather | bytes 327680 | tf_op jit(solution)/shard_map/all_gather | solution.py:34
  95.2 3.6 collective-permute-start.2
  98.8 3.5 collective-permute-done.1
  104.2 12.5 %all_gather.47 = f32[256,256]{1,0:T(8,128)S(1)} all-gather(f32[64,256]{1,0:T(8,128)S(1)} %fusion.92), channel_id=1, replica_groups=mesh['leaf'=128,'sep'=4] {'sep'}, dimensions={0}, use_global_device_ids=true | all-gather | bytes 327680 | tf_op jit(solution)/shard_map/all_gather | solution.py:34
  117.8 3.4 collective-permute-start.3
  123.7 4.8 collective-permute-done.3
  128.5 4.6 collective-permute-done.4
  133.2 12.3 %all_gather.48 = f32[256,256]{1,0:T(8,128)S(1)} all-gather(f32[64,256]{1,0:T(8,128)S(1)} %fusion.90), channel_id=1, replica_groups=mesh['leaf'=128,'sep'=4] {'sep'}, dimensions={0}, use_global_device_ids=true | all-gather | bytes 327680 | tf_op jit(solution)/shard_map/all_gather | solution.py:34
  146.5 6.2 %collective-permute-start.5 = (f32[64,4,256]{2,0,1:T(8,128)S(1)}, f32[64,4,256]{2,0,1:T(8,128)S(1)}, u32[]{:S(2)}, u32[]{:S(2)}) collective-permute-start(f32[64,4,256]{2,0,1:T(8,128)S(1)} %slice.692), channel_id=1, source_target_pairs={{0,16},{4,20},{8,24},{12,28},{16,32},{20,36},{24,40},{28,44},{32,4... | collective-permute-start | bytes 786440 | tf_op jit(solution)/shard_map/ppermute | solution.py:12
  154.0 5.3 %collective-permute-done.5 = f32[64,4,256]{2,0,1:T(8,128)S(1)} collective-permute-done((f32[64,4,256]{2,0,1:T(8,128)S(1)}, f32[64,4,256]{2,0,1:T(8,128)S(1)}, u32[]{:S(2)}, u32[]{:S(2)}) %collective-permute-start.5) | collective-permute-done | bytes 262176 | tf_op jit(solution)/shard_map/ppermute | solution.py:12
  159.3 5.3 %collective-permute-done.6 = f32[64,4,256]{2,0,1:T(8,128)} collective-permute-done((f32[64,4,256]{2,0,1:T(8,128)S(1)}, f32[64,4,256]{2,0,1:T(8,128)}, u32[]{:S(2)}, u32[]{:S(2)}) %collective-permute-start.6) | collective-permute-done | bytes 262176 | tf_op jit(solution)/shard_map/ppermute | solution.py:12
  165.7 12.3 %all_gather.49 = f32[256,256]{1,0:T(8,128)S(1)} all-gather(f32[64,256]{1,0:T(8,128)S(1)} %fusion.88), channel_id=1, replica_groups=mesh['leaf'=128,'sep'=4] {'sep'}, dimensions={0}, use_global_device_ids=true | all-gather | bytes 327680 | tf_op jit(solution)/shard_map/all_gather | solution.py:34
  178.9 3.6 collective-permute-start.7
  183.9 3.3 collective-permute-done.7
  187.2 12.7 %collective-permute-done.8 = f32[64,3,256]{2,0,1:T(8,128)S(1)} collective-permute-done((f32[64,3,256]{2,0,1:T(8,128)S(1)}, f32[64,3,256]{2,0,1:T(8,128)S(1)}, u32[]{:S(2)}, u32[]{:S(2)}) %collective-permute-start.8) | collective-permute-done | bytes 196640 | tf_op jit(solution)/shard_map/ppermute | solution.py:12
  199.9 12.3 %all_gather.50 = f32[256,256]{1,0:T(8,128)S(1)} all-gather(f32[64,256]{1,0:T(8,128)S(1)} %fusion.86), channel_id=1, replica_groups=mesh['leaf'=128,'sep'=4] {'sep'}, dimensions={0}, use_global_device_ids=true | all-gather | bytes 327680 | tf_op jit(solution)/shard_map/all_gather | solution.py:34
  213.2 4.5 collective-permute-start.9
  220.2 4.7 collective-permute-done.10
  225.8 12.3 %all_gather.51 = f32[256,256]{1,0:T(8,128)S(1)} all-gather(f32[64,256]{1,0:T(8,128)S(1)} %fusion.85), channel_id=1, replica_groups=mesh['leaf'=128,'sep'=4] {'sep'}, dimensions={0}, use_global_device_ids=true | all-gather | bytes 327680 | tf_op jit(solution)/shard_map/all_gather | solution.py:34
  239.0 3.7 collective-permute-start.11
  244.6 5.2 collective-permute-done.12
  249.8 12.4 %all_gather.52 = f32[256,256]{1,0:T(8,128)S(1)} all-gather(f32[64,256]{1,0:T(8,128)S(1)} %bitcast_subtract_fusion), channel_id=1, replica_groups=mesh['leaf'=128,'sep'=4] {'sep'}, dimensions={0}, use_global_device_ids=true | all-gather | bytes 327680 | tf_op jit(solution)/shard_map/all_gather | solution.py:34
  263.5 4.7 collective-permute-start.13
  270.1 5.2 collective-permute-done.14
  275.3 12.7 %all-gather.1 = f32[256,1,256]{2,1,0:T(1,128)S(1)} all-gather(f32[64,1,256]{2,1,0:T(1,128)S(1)} %copy.70), channel_id=3, replica_groups=mesh['leaf'=128,'sep'=4] {'sep'}, dimensions={0}, use_global_device_ids=true | all-gather | bytes 327680 | tf_op jit(solution)/shard_map/all_gather | solution.py:34
  289.3 3.8 collective-permute-start.15
  295.6 4.4 collective-permute-done.16
  300.1 12.3 %all-gather.2 = f32[256,1,256]{2,1,0:T(1,128)S(1)} all-gather(f32[64,1,256]{2,1,0:T(1,128)S(1)} %copy.71), channel_id=4, replica_groups=mesh['leaf'=128,'sep'=4] {'sep'}, dimensions={0}, use_global_device_ids=true | all-gather | bytes 327680 | tf_op jit(solution)/shard_map/all_gather | solution.py:34
  313.6 6.9 %collective-permute-start.17 = (f32[64,3,256]{2,0,1:T(8,128)S(1)}, f32[64,3,256]{2,0,1:T(8,128)S(1)}, u32[]{:S(2)}, u32[]{:S(2)}) collective-permute-start(f32[64,3,256]{2,0,1:T(8,128)S(1)} %slice.705), channel_id=1, source_target_pairs={{0,32},{4,36},{8,40},{12,44},{16,48},{20,52},{24,56},{28,60},{32,6... | collective-permute-start | bytes 589832 | tf_op jit(solution)/shard_map/ppermute | solution.py:12
  321.9 2.9 collective-permute-done.17
  324.8 12.8 %collective-permute-done.18 = f32[64,3,256]{2,0,1:T(8,128)S(1)} collective-permute-done((f32[64,3,256]{2,0,1:T(8,128)S(1)}, f32[64,3,256]{2,0,1:T(8,128)S(1)}, u32[]{:S(2)}, u32[]{:S(2)}) %collective-permute-start.18) | collective-permute-done | bytes 196640 | tf_op jit(solution)/shard_map/ppermute | solution.py:12
  337.7 12.8 %all-gather.3 = f32[256,1,256]{2,1,0:T(1,128)S(1)} all-gather(f32[64,1,256]{2,1,0:T(1,128)S(1)} %copy.72), channel_id=5, replica_groups=mesh['leaf'=128,'sep'=4] {'sep'}, dimensions={0}, use_global_device_ids=true | all-gather | bytes 327680 | tf_op jit(solution)/shard_map/all_gather | solution.py:34
  355.1 2.6 collective-permute-done.19
  357.7 10.0 %collective-permute-done.20 = f32[64,4,256]{2,0,1:T(8,128)S(1)} collective-permute-done((f32[64,4,256]{2,0,1:T(8,128)S(1)}, f32[64,4,256]{2,0,1:T(8,128)S(1)}, u32[]{:S(2)}, u32[]{:S(2)}) %collective-permute-start.20) | collective-permute-done | bytes 262176 | tf_op jit(solution)/shard_map/ppermute | solution.py:12
  367.9 12.3 %all-gather.4 = f32[256,1,256]{2,1,0:T(1,128)S(1)} all-gather(f32[64,1,256]{2,1,0:T(1,128)S(1)} %copy.73), channel_id=6, replica_groups=mesh['leaf'=128,'sep'=4] {'sep'}, dimensions={0}, use_global_device_ids=true | all-gather | bytes 327680 | tf_op jit(solution)/shard_map/all_gather | solution.py:34
  382.1 3.9 collective-permute-start.21
  388.0 3.1 collective-permute-done.21
  391.1 5.2 %collective-permute-done.22 = f32[64,5,256]{2,0,1:T(8,128)S(1)} collective-permute-done((f32[64,5,256]{2,0,1:T(8,128)S(1)}, f32[64,5,256]{2,0,1:T(8,128)S(1)}, u32[]{:S(2)}, u32[]{:S(2)}) %collective-permute-start.22) | collective-permute-done | bytes 327712 | tf_op jit(solution)/shard_map/ppermute | solution.py:12
  396.6 12.3 %all-gather.5 = f32[256,1,256]{2,1,0:T(1,128)S(1)} all-gather(f32[64,1,256]{2,1,0:T(1,128)S(1)} %copy.74), channel_id=7, replica_groups=mesh['leaf'=128,'sep'=4] {'sep'}, dimensions={0}, use_global_device_ids=true | all-gather | bytes 327680 | tf_op jit(solution)/shard_map/all_gather | solution.py:34
  412.6 3.6 collective-permute-start.24
  416.3 3.5 collective-permute-done.23
  421.8 12.3 %all-gather.6 = f32[256,1,256]{2,1,0:T(1,128)S(1)} all-gather(f32[64,1,256]{2,1,0:T(1,128)S(1)} %copy.75), channel_id=8, replica_groups=mesh['leaf'=128,'sep'=4] {'sep'}, dimensions={0}, use_global_device_ids=true | all-gather | bytes 327680 | tf_op jit(solution)/shard_map/all_gather | solution.py:34
  437.3 6.0 %collective-permute-done.25 = f32[64,7,256]{2,0,1:T(8,128)S(1)} collective-permute-done((f32[64,7,256]{2,0,1:T(8,128)S(1)}, f32[64,7,256]{2,0,1:T(8,128)S(1)}, u32[]{:S(2)}, u32[]{:S(2)}) %collective-permute-start.25) | collective-permute-done | bytes 458784 | tf_op jit(solution)/shard_map/ppermute | solution.py:12
  444.5 32.9 %all-gather.9.cloned.1.call-done = f32[256,7,256]{2,0,1:T(8,128)} async-done(((f32[64,7,256]{2,0,1:T(8,128)}), f32[256,7,256]{2,0,1:T(8,128)}) %all-gather.9.cloned.1.call-update) | async-done | bytes 1835024 | tf_op jit(solution)/shard_map/all_gather | solution.py:34
  484.2 25.8 %reduce-scatter.7.cloned.1.call-done = f32[160,256]{1,0:T(8,128)} async-done(((f32[640,256]{1,0:T(8,128)}), f32[160,256]{1,0:T(8,128)}) %reduce-scatter.7.cloned.1.call-update) | async-done | bytes 163856
  (155 shorter events, 69.4 us)
Async XLA Ops:
  7.2 16.1 %copy-start = (f32[1,896,160]{1,2,0:T(8,128)S(1)}, f32[1,896,160]{1,2,0:T(8,128)}, u32[]{:S(2)}) copy-start(f32[1,896,160]{1,2,0:T(8,128)} %param.64) | copy-start | bytes 1720324
  7.2 60.4 %reduce-scatter.5.cloned.1.call-start = ((), (), s32[]{:S(2)}) async-start(), calls=%async_computation.2 | async-start | bytes 2621440 | tf_op jit(solution)/shard_map/reduce_scatter | solution.py:73
  23.3 1.4 copy-start.10
  24.7 3.1 copy-start.8
  27.8 52.0 %copy-start.3 = (f32[1,64,256]{2,1,0:T(8,128)S(1)}, f32[1,64,256]{2,1,0:T(8,128)}, u32[]{:S(2)}) copy-start(f32[1,64,256]{2,1,0:T(8,128)} %param.67) | copy-start | bytes 196612
  27.8 64.4 %copy-start.1 = (f32[1,256,256]{2,1,0:T(8,128)S(1)}, f32[1,256,256]{2,1,0:T(8,128)}, u32[]{:S(2)}) copy-start(f32[1,256,256]{2,1,0:T(8,128)} %param.68) | copy-start | bytes 786436
  27.8 65.0 %copy-start.2 = (f32[1,256,256]{2,1,0:T(8,128)S(1)}, f32[1,256,256]{2,1,0:T(8,128)}, u32[]{:S(2)}) copy-start(f32[1,256,256]{2,1,0:T(8,128)} %param.69) | copy-start | bytes 786436
  27.8 449.6 %all-gather.9.cloned.1.call-start = ((), (), s32[]{:S(2)}) async-start(), calls=%async_computation.3 | async-start | bytes 2293760 | tf_op jit(solution)/shard_map/all_gather | solution.py:34
  68.8 9.8 %collective-permute-start = (f32[64,7,256]{2,0,1:T(8,128)S(1)}, f32[64,7,256]{2,0,1:T(8,128)S(1)}, u32[]{:S(2)}, u32[]{:S(2)}) collective-permute-start(f32[64,7,256]{2,0,1:T(8,128)S(1)} %copy.67), channel_id=1, source_target_pairs={{0,4},{4,8},{8,12},{12,16},{16,20},{20,24},{24,28},{28,32},{32,36}... | collective-permute-start | bytes 1376264 | tf_op jit(solution)/shard_map/ppermute | solution.py:12
  93.2 9.1 %collective-permute-start.1 = (f32[64,6,256]{2,0,1:T(8,128)S(1)}, f32[64,6,256]{2,0,1:T(8,128)S(1)}, u32[]{:S(2)}, u32[]{:S(2)}) collective-permute-start(f32[64,6,256]{2,0,1:T(8,128)S(1)} %slice.686), channel_id=1, source_target_pairs={{0,4},{4,8},{8,12},{12,16},{16,20},{20,24},{24,28},{28,32},{32,36}... | collective-permute-start | bytes 1179656 | tf_op jit(solution)/shard_map/ppermute | solution.py:12
  95.2 8.9 %collective-permute-start.2 = (f32[64,6,256]{2,0,1:T(8,128)S(1)}, f32[64,6,256]{2,0,1:T(8,128)S(1)}, u32[]{:S(2)}, u32[]{:S(2)}) collective-permute-start(f32[64,6,256]{2,0,1:T(8,128)S(1)} %slice.686), channel_id=1, source_target_pairs={{4,0},{8,4},{12,8},{16,12},{20,16},{24,20},{28,24},{32,28},{36,32}... | collective-permute-start | bytes 1179656 | tf_op jit(solution)/shard_map/ppermute | solution.py:12
  117.8 10.7 %collective-permute-start.3 = (f32[64,5,256]{2,0,1:T(8,128)S(1)}, f32[64,5,256]{2,0,1:T(8,128)S(1)}, u32[]{:S(2)}, u32[]{:S(2)}) collective-permute-start(f32[64,5,256]{2,0,1:T(8,128)S(1)} %slice.689), channel_id=1, source_target_pairs={{0,8},{4,12},{8,16},{12,20},{16,24},{20,28},{24,32},{28,36},{32,40... | collective-permute-start | bytes 983048 | tf_op jit(solution)/shard_map/ppermute | solution.py:12
  121.2 11.9 %collective-permute-start.4 = (f32[64,5,256]{2,0,1:T(8,128)S(1)}, f32[64,5,256]{2,0,1:T(8,128)S(1)}, u32[]{:S(2)}, u32[]{:S(2)}) collective-permute-start(f32[64,5,256]{2,0,1:T(8,128)S(1)} %slice.689), channel_id=1, source_target_pairs={{8,0},{12,4},{16,8},{20,12},{24,16},{28,20},{32,24},{36,28},{40,32... | collective-permute-start | bytes 983048 | tf_op jit(solution)/shard_map/ppermute | solution.py:12
  146.5 12.8 %collective-permute-start.5 = (f32[64,4,256]{2,0,1:T(8,128)S(1)}, f32[64,4,256]{2,0,1:T(8,128)S(1)}, u32[]{:S(2)}, u32[]{:S(2)}) collective-permute-start(f32[64,4,256]{2,0,1:T(8,128)S(1)} %slice.692), channel_id=1, source_target_pairs={{0,16},{4,20},{8,24},{12,28},{16,32},{20,36},{24,40},{28,44},{32,4... | collective-permute-start | bytes 786440 | tf_op jit(solution)/shard_map/ppermute | solution.py:12
  152.7 12.0 %collective-permute-start.6 = (f32[64,4,256]{2,0,1:T(8,128)S(1)}, f32[64,4,256]{2,0,1:T(8,128)}, u32[]{:S(2)}, u32[]{:S(2)}) collective-permute-start(f32[64,4,256]{2,0,1:T(8,128)S(1)} %slice.692), channel_id=1, source_target_pairs={{16,0},{20,4},{24,8},{28,12},{32,16},{36,20},{40,24},{44,28},{48,3... | collective-permute-start | bytes 786440 | tf_op jit(solution)/shard_map/ppermute | solution.py:12
  178.9 8.2 %collective-permute-start.7 = (f32[64,3,256]{2,0,1:T(8,128)S(1)}, f32[64,3,256]{2,0,1:T(8,128)S(1)}, u32[]{:S(2)}, u32[]{:S(2)}) collective-permute-start(f32[64,3,256]{2,0,1:T(8,128)S(1)} %slice.695), channel_id=1, source_target_pairs={{0,32},{4,36},{8,40},{12,44},{16,48},{20,52},{24,56},{28,60},{32,6... | collective-permute-start | bytes 589832 | tf_op jit(solution)/shard_map/ppermute | solution.py:12
  182.6 17.3 %collective-permute-start.8 = (f32[64,3,256]{2,0,1:T(8,128)S(1)}, f32[64,3,256]{2,0,1:T(8,128)S(1)}, u32[]{:S(2)}, u32[]{:S(2)}) collective-permute-start(f32[64,3,256]{2,0,1:T(8,128)S(1)} %slice.695), channel_id=1, source_target_pairs={{32,0},{36,4},{40,8},{44,12},{48,16},{52,20},{56,24},{60,28},{64,3... | collective-permute-start | bytes 589832 | tf_op jit(solution)/shard_map/ppermute | solution.py:12
  213.2 7.0 %collective-permute-start.9 = (f32[64,2,256]{2,0,1:T(8,128)S(1)}, f32[64,2,256]{2,0,1:T(8,128)S(1)}, u32[]{:S(2)}, u32[]{:S(2)}) collective-permute-start(f32[64,2,256]{2,0,1:T(8,128)S(1)} %slice.698), channel_id=1, source_target_pairs={{0,64},{4,68},{8,72},{12,76},{16,80},{20,84},{24,88},{28,92},{32,9... | collective-permute-start | bytes 393224 | tf_op jit(solution)/shard_map/ppermute | solution.py:12
  217.7 7.2 %collective-permute-start.10 = (f32[64,2,256]{2,0,1:T(8,128)S(1)}, f32[64,2,256]{2,0,1:T(8,128)}, u32[]{:S(2)}, u32[]{:S(2)}) collective-permute-start(f32[64,2,256]{2,0,1:T(8,128)S(1)} %slice.698), channel_id=1, source_target_pairs={{64,0},{68,4},{72,8},{76,12},{80,16},{84,20},{88,24},{92,28},{96,3... | collective-permute-start | bytes 393224 | tf_op jit(solution)/shard_map/ppermute | solution.py:12
  239.0 5.6 %collective-permute-start.11 = (f32[64,1,256]{2,0,1:T(8,128)S(1)}, f32[64,1,256]{2,0,1:T(8,128)S(1)}, u32[]{:S(2)}, u32[]{:S(2)}) collective-permute-start(f32[64,1,256]{2,0,1:T(8,128)S(1)} %slice_add_fusion), channel_id=1, source_target_pairs={{0,128},{4,132},{8,136},{12,140},{16,144},{20,148},{24,152},{28,15... | collective-permute-start | bytes 196616 | tf_op jit(solution)/shard_map/ppermute | solution.py:12
  242.7 7.1 %collective-permute-start.12 = (f32[64,1,256]{2,0,1:T(8,128)S(1)}, f32[64,1,256]{2,0,1:T(8,128)S(1)}, u32[]{:S(2)}, u32[]{:S(2)}) collective-permute-start(f32[64,1,256]{2,0,1:T(8,128)S(1)} %slice_add_fusion), channel_id=1, source_target_pairs={{128,0},{132,4},{136,8},{140,12},{144,16},{148,20},{152,24},{156,2... | collective-permute-start | bytes 196616 | tf_op jit(solution)/shard_map/ppermute | solution.py:12
  263.5 6.6 %collective-permute-start.13 = (f32[64,1,256]{2,0,1:T(8,128)S(1)}, f32[64,1,256]{2,0,1:T(8,128)S(1)}, u32[]{:S(2)}, u32[]{:S(2)}) collective-permute-start(f32[64,1,256]{2,0,1:T(8,128)S(1)} %select_bitcast_fusion), channel_id=1, source_target_pairs={{0,128},{4,132},{8,136},{12,140},{16,144},{20,148},{24,152},{28,15... | collective-permute-start | bytes 196616 | tf_op jit(solution)/shard_map/ppermute | solution.py:12
  268.2 7.1 %collective-permute-start.14 = (f32[64,1,256]{2,0,1:T(8,128)S(1)}, f32[64,1,256]{2,0,1:T(8,128)S(1)}, u32[]{:S(2)}, u32[]{:S(2)}) collective-permute-start(f32[64,1,256]{2,0,1:T(8,128)S(1)} %select_bitcast_fusion), channel_id=1, source_target_pairs={{128,0},{132,4},{136,8},{140,12},{144,16},{148,20},{152,24},{156,2... | collective-permute-start | bytes 196616 | tf_op jit(solution)/shard_map/ppermute | solution.py:12
  289.3 6.3 %collective-permute-start.15 = (f32[64,2,256]{2,0,1:T(8,128)S(1)}, f32[64,2,256]{2,0,1:T(8,128)S(1)}, u32[]{:S(2)}, u32[]{:S(2)}) collective-permute-start(f32[64,2,256]{2,0,1:T(8,128)S(1)} %slice.702), channel_id=1, source_target_pairs={{0,64},{4,68},{8,72},{12,76},{16,80},{20,84},{24,88},{28,92},{32,9... | collective-permute-start | bytes 393224 | tf_op jit(solution)/shard_map/ppermute | solution.py:12
  293.1 6.9 %collective-permute-start.16 = (f32[64,2,256]{2,0,1:T(8,128)S(1)}, f32[64,2,256]{2,0,1:T(8,128)S(1)}, u32[]{:S(2)}, u32[]{:S(2)}) collective-permute-start(f32[64,2,256]{2,0,1:T(8,128)S(1)} %slice.702), channel_id=1, source_target_pairs={{64,0},{68,4},{72,8},{76,12},{80,16},{84,20},{88,24},{92,28},{96,3... | collective-permute-start | bytes 393224 | tf_op jit(solution)/shard_map/ppermute | solution.py:12
  313.6 11.1 %collective-permute-start.17 = (f32[64,3,256]{2,0,1:T(8,128)S(1)}, f32[64,3,256]{2,0,1:T(8,128)S(1)}, u32[]{:S(2)}, u32[]{:S(2)}) collective-permute-start(f32[64,3,256]{2,0,1:T(8,128)S(1)} %slice.705), channel_id=1, source_target_pairs={{0,32},{4,36},{8,40},{12,44},{16,48},{20,52},{24,56},{28,60},{32,6... | collective-permute-start | bytes 589832 | tf_op jit(solution)/shard_map/ppermute | solution.py:12
  320.6 17.0 %collective-permute-start.18 = (f32[64,3,256]{2,0,1:T(8,128)S(1)}, f32[64,3,256]{2,0,1:T(8,128)S(1)}, u32[]{:S(2)}, u32[]{:S(2)}) collective-permute-start(f32[64,3,256]{2,0,1:T(8,128)S(1)} %slice.705), channel_id=1, source_target_pairs={{32,0},{36,4},{40,8},{44,12},{48,16},{52,20},{56,24},{60,28},{64,3... | collective-permute-start | bytes 589832 | tf_op jit(solution)/shard_map/ppermute | solution.py:12
  352.4 5.2 %collective-permute-start.19 = (f32[64,4,256]{2,0,1:T(8,128)S(1)}, f32[64,4,256]{2,0,1:T(8,128)S(1)}, u32[]{:S(2)}, u32[]{:S(2)}) collective-permute-start(f32[64,4,256]{2,0,1:T(8,128)S(1)} %slice.708), channel_id=1, source_target_pairs={{0,16},{4,20},{8,24},{12,28},{16,32},{20,36},{24,40},{28,44},{32,4... | collective-permute-start | bytes 786440 | tf_op jit(solution)/shard_map/ppermute | solution.py:12
  353.8 13.9 %collective-permute-start.20 = (f32[64,4,256]{2,0,1:T(8,128)S(1)}, f32[64,4,256]{2,0,1:T(8,128)S(1)}, u32[]{:S(2)}, u32[]{:S(2)}) collective-permute-start(f32[64,4,256]{2,0,1:T(8,128)S(1)} %slice.708), channel_id=1, source_target_pairs={{16,0},{20,4},{24,8},{28,12},{32,16},{36,20},{40,24},{44,28},{48,3... | collective-permute-start | bytes 786440 | tf_op jit(solution)/shard_map/ppermute | solution.py:12
  382.1 9.0 %collective-permute-start.21 = (f32[64,5,256]{2,0,1:T(8,128)S(1)}, f32[64,5,256]{2,0,1:T(8,128)S(1)}, u32[]{:S(2)}, u32[]{:S(2)}) collective-permute-start(f32[64,5,256]{2,0,1:T(8,128)S(1)} %slice.711), channel_id=1, source_target_pairs={{0,8},{4,12},{8,16},{12,20},{16,24},{20,28},{24,32},{28,36},{32,40... | collective-permute-start | bytes 983048 | tf_op jit(solution)/shard_map/ppermute | solution.py:12
  386.0 10.3 %collective-permute-start.22 = (f32[64,5,256]{2,0,1:T(8,128)S(1)}, f32[64,5,256]{2,0,1:T(8,128)S(1)}, u32[]{:S(2)}, u32[]{:S(2)}) collective-permute-start(f32[64,5,256]{2,0,1:T(8,128)S(1)} %slice.711), channel_id=1, source_target_pairs={{8,0},{12,4},{16,8},{20,12},{24,16},{28,20},{32,24},{36,28},{40,32... | collective-permute-start | bytes 983048 | tf_op jit(solution)/shard_map/ppermute | solution.py:12
  410.7 9.1 %collective-permute-start.23 = (f32[64,6,256]{2,0,1:T(8,128)S(1)}, f32[64,6,256]{2,0,1:T(8,128)S(1)}, u32[]{:S(2)}, u32[]{:S(2)}) collective-permute-start(f32[64,6,256]{2,0,1:T(8,128)S(1)} %slice.714), channel_id=1, source_target_pairs={{0,4},{4,8},{8,12},{12,16},{16,20},{20,24},{24,28},{28,32},{32,36}... | collective-permute-start | bytes 1179656 | tf_op jit(solution)/shard_map/ppermute | solution.py:12
  412.6 8.9 %collective-permute-start.24 = (f32[64,6,256]{2,0,1:T(8,128)S(1)}, f32[64,6,256]{2,0,1:T(8,128)S(1)}, u32[]{:S(2)}, u32[]{:S(2)}) collective-permute-start(f32[64,6,256]{2,0,1:T(8,128)S(1)} %slice.714), channel_id=1, source_target_pairs={{4,0},{8,4},{12,8},{16,12},{20,16},{24,20},{28,24},{32,28},{36,32}... | collective-permute-start | bytes 1179656 | tf_op jit(solution)/shard_map/ppermute | solution.py:12
  434.1 10.3 %copy-start.11 = (s32[1,7]{1,0:T(1,128)S(1)}, s32[1,7]{1,0:T(1,128)}, u32[]{:S(2)}) copy-start(s32[1,7]{1,0:T(1,128)} %param.66) | copy-start | bytes 88
  434.1 43.2 %copy-start.9 = (s32[896]{0:T(1024)S(1)}, s32[896]{0:T(1024)}, u32[]{:S(2)}) copy-start(s32[896]{0:T(1024)} %copy-done.8) | copy-start | bytes 10756
  435.4 7.9 %collective-permute-start.25 = (f32[64,7,256]{2,0,1:T(8,128)S(1)}, f32[64,7,256]{2,0,1:T(8,128)S(1)}, u32[]{:S(2)}, u32[]{:S(2)}) collective-permute-start(f32[64,7,256]{2,0,1:T(8,128)S(1)} %get-tuple-element.328), channel_id=1, source_target_pairs={{4,0},{8,4},{12,8},{16,12},{20,16},{24,20},{28,24},{32,28},{36,32}... | collective-permute-start | bytes 1376264 | tf_op jit(solution)/shard_map/ppermute | solution.py:12
  444.2 65.8 %reduce-scatter.7.cloned.1.call-start = ((), (), s32[]{:S(2)}) async-start(), calls=%async_computation.4 | async-start | bytes 819200
  444.5 36.0 %copy-start.4 = (f32[1,160,640]{2,1,0:T(8,128)S(1)}, f32[1,160,640]{2,1,0:T(8,128)}, u32[]{:S(2)}) copy-start(f32[1,160,640]{2,1,0:T(8,128)} %param.63) | copy-start | bytes 1228804
  481.4 1.5 copy-start.5
  481.4 1.6 copy-start.6
  481.4 1.7 copy-start.7
Sparse Core Ops, SparseCore 0:
  27.9 39.6 reduce-scatter.4
  444.3 33.0 all-gather.8
  482.7 27.2 reduce-scatter.6
where the time goes:
time: 519 us; the launch traced here: 518 us
  waiting for transfers between devices  218 us (42%)
  blocking collectives  175 us (34%)
  starting transfers between devices  72.1 us (14%)
  matrix products  21.9 us (4%)
  between operations  15 us (3%)
  local copies, waits for them, and re-layouts  8.57 us (2%)
  other arithmetic  7.86 us (2%)
    all_gather x13, blocking collectives, sep_rows(): return lax.all_gather(payload, 'sep', axis=0, tiled=True)  161 us
    ppermute x26, waiting for transfers between devices, passed_along(): return lax.ppermute(x, axis, pairs)  120 us
    ppermute x26, starting transfers between devices, passed_along(): return lax.ppermute(x, axis, pairs)  71.8 us
    reduce_scatter x1, waiting for transfers between devices, per_device(): lax.psum_scatter(densified, 'sep', scatter_dimension=0, tiled=True)  39.7 us
    all_gather x1, waiting for transfers between devices, sep_rows(): return lax.all_gather(payload, 'sep', axis=0, tiled=True)  32.9 us
    unnamed x4, waiting for transfers between devices  25.8 us
    all_gather x1, blocking collectives, per_device(): lax.all_gather(source, 'sep', axis=0, tiled=True)  13.7 us
  transfers between devices with their start and end apart: 29, of which 29 were waited for; matrix products, arithmetic and copies ran while one was open for 0% of the time, Pallas kernels for 0%

commit v1 on v0

--- a/solution.py
+++ b/solution.py
@@ -1,9 +1,22 @@
+import functools
 import jax
 import jax.numpy as jnp
 from jax import lax
 from jax.sharding import PartitionSpec as P
 
 highest = lax.Precision.HIGHEST
+
+
+def unite_ticks(sample, mesh_name, d0):
+    num = lax.axis_size(mesh_name)
+    log = list(map(lambda hop_no: num if hop_no == d0 else 1, range(sample.ndim)))
+    all_rows = lax.all_to_all(
+        jnp.tile(sample, log), mesh_name, split_axis=d0, concat_axis=d0, tiled=True
+    )
+    return all_rows
+
+
+pass_rings = functools.partial(unite_ticks, mesh_name="sep", d0=0)
 
 
 def passed_along(x, axis, by):
@@ -31,7 +44,7 @@
 
 
 def sep_rows(payload):
-    return lax.all_gather(payload, "sep", axis=0, tiled=True)
+    return pass_rings(payload)
 
 
 def per_device(

time: 519 us -> 493 us (0.950)
  blocking collectives: 175 us -> 86.3 us
  starting transfers between devices: 72.1 us -> 108 us
  waiting for transfers between devices: 218 us -> 234 us
  local copies, waits for them, and re-layouts: 8.57 us -> 13.8 us
    all_gather x13 -> x0, blocking collectives: 161 us -> none  [sep_rows(): return lax.all_gather(payload, 'sep', axis=0, tiled=True)]
    all_to_all x0 -> x8, blocking collectives: none -> 72.6 us  [unite_ticks(): lax.all_to_all(jnp.tile(sample, log), mesh_name, split_axis=d0, concat_ax...]
    all_to_all x0 -> x6, waiting for transfers between devices: none -> 60 us  [unite_ticks(): lax.all_to_all(jnp.tile(sample, log), mesh_name, split_axis=d0, concat_ax...]
    all_gather x1 -> x0, waiting for transfers between devices: 32.9 us -> none  [sep_rows(): return lax.all_gather(payload, 'sep', axis=0, tiled=True)]
    all_to_all x0 -> x6, starting transfers between devices: none -> 22.1 us  [unite_ticks(): lax.all_to_all(jnp.tile(sample, log), mesh_name, split_axis=d0, concat_ax...]
    ppermute x26, starting transfers between devices: 71.8 us -> 85.9 us  [passed_along(): return lax.ppermute(x, axis, pairs)]
    ppermute x26, waiting for transfers between devices: 120 us -> 113 us  [passed_along(): return lax.ppermute(x, axis, pairs)]
    another operation x0 -> x19, local copies, waits for them, and re-layouts: none -> 5.38 us  [unite_ticks(): jnp.tile(sample, log)]
  transfers between devices with their start and end apart: 29 -> 34, of which waited for: 29 -> 34; matrix products, arithmetic and copies ran while one was open for 0% -> 0% of each run, Pallas kernels for 0% -> 0%
where the time goes in v1:
time: 493 us; the launch traced here: 491 us
  waiting for transfers between devices  234 us (47%)
  starting transfers between devices  108 us (22%)
  blocking collectives  86.3 us (18%)
  matrix products  22.7 us (5%)
  between operations  15.3 us (3%)
  local copies, waits for them, and re-layouts  13.8 us (3%)
  other arithmetic  11 us (2%)
    ppermute x26, waiting for transfers between devices, passed_along(): return lax.ppermute(x, axis, pairs)  113 us
    ppermute x26, starting transfers between devices, passed_along(): return lax.ppermute(x, axis, pairs)  85.9 us
    all_to_all x8, blocking collectives, unite_ticks(): lax.all_to_all(jnp.tile(sample, log), mesh_name, split_axis=d0, concat_ax...  72.6 us
    all_to_all x6, waiting for transfers between devices, unite_ticks(): lax.all_to_all(jnp.tile(sample, log), mesh_name, split_axis=d0, concat_ax...  60 us
    reduce_scatter x1, waiting for transfers between devices, per_device(): lax.psum_scatter(densified, 'sep', scatter_dimension=0, tiled=True)  39.8 us
    all_to_all x6, starting transfers between devices, unite_ticks(): lax.all_to_all(jnp.tile(sample, log), mesh_name, split_axis=d0, concat_ax...  22.1 us
    unnamed x3, waiting for transfers between devices  21.8 us
    all_gather x1, blocking collectives, per_device(): lax.all_gather(source, 'sep', axis=0, tiled=True)  13.7 us
  transfers between devices with their start and end apart: 34, of which 34 were waited for; matrix products, arithmetic and copies ran while one was open for 0% of the time, Pallas kernels for 0%

profile of v1, /device:TPU:8, one launch (start us, length us, event | category | flops | bytes accessed | tf_op | source)
XLA Modules:
  0.0 491.4 jit_solution(8253437363581430895)
XLA Ops:
  7.2 13.7 %all-gather = f32[1,640,256]{2,1,0:T(8,128)S(1)} all-gather(f32[1,160,256]{2,1,0:T(8,128)} %param.62), channel_id=2, replica_groups=mesh['leaf'=128,'sep'=4] {'sep'}, dimensions={1}, use_global_device_ids=true | all-gather | bytes 819200 | tf_op jit(solution)/shard_map/all_gather | solution.py:72
  27.8 39.8 %reduce-scatter.5.cloned.1.call-done = f32[64,7,256]{2,1,0:T(8,128)} async-done(((f32[256,7,256]{2,1,0:T(8,128)}), f32[64,7,256]{2,1,0:T(8,128)}) %reduce-scatter.5.cloned.1.call-update) | async-done | bytes 458768 | tf_op jit(solution)/shard_map/reduce_scatter | solution.py:86
  70.7 7.9 %collective-permute-done = f32[64,7,256]{2,0,1:T(8,128)S(1)} collective-permute-done((f32[64,7,256]{2,0,1:T(8,128)S(1)}, f32[64,7,256]{2,0,1:T(8,128)S(1)}, u32[]{:S(2)}, u32[]{:S(2)}) %collective-permute-start) | collective-permute-done | bytes 458784 | tf_op jit(solution)/shard_map/ppermute | solution.py:25
  80.5 3.4 all-to-all-start
  84.0 6.6 %all-to-all-done = f32[4,64,256]{2,1,0:T(8,128)S(1)} async-done(((f32[4,64,256]{2,1,0:T(8,128)}), f32[4,64,256]{2,1,0:T(8,128)S(1)}, u32[]{:S(2)}, u32[]{:S(2)}) %all-to-all-start) | async-done | bytes 262176 | tf_op jit(solution)/shard_map/all_to_all | solution.py:13
  93.6 3.6 collective-permute-start.2
  97.2 3.5 collective-permute-done.1
  104.3 3.4 all-to-all-start.1
  107.8 7.1 %all-to-all-done.1 = f32[4,64,256]{2,1,0:T(8,128)S(1)} async-done(((f32[4,64,256]{2,1,0:T(8,128)}), f32[4,64,256]{2,1,0:T(8,128)S(1)}, u32[]{:S(2)}, u32[]{:S(2)}) %all-to-all-start.1) | async-done | bytes 262176 | tf_op jit(solution)/shard_map/all_to_all | solution.py:13
  115.9 2.9 collective-permute-start.3
  118.8 3.0 collective-permute-start.4
  121.8 6.3 %collective-permute-done.3 = f32[64,5,256]{2,0,1:T(8,128)S(1)} collective-permute-done((f32[64,5,256]{2,0,1:T(8,128)S(1)}, f32[64,5,256]{2,0,1:T(8,128)S(1)}, u32[]{:S(2)}, u32[]{:S(2)}) %collective-permute-start.3) | collective-permute-done | bytes 327712 | tf_op jit(solution)/shard_map/ppermute | solution.py:25
  131.1 3.4 all-to-all-start.2
  134.6 6.9 %all-to-all-done.2 = f32[4,64,256]{2,1,0:T(8,128)S(1)} async-done(((f32[4,64,256]{2,1,0:T(8,128)}), f32[4,64,256]{2,1,0:T(8,128)S(1)}, u32[]{:S(2)}, u32[]{:S(2)}) %all-to-all-start.2) | async-done | bytes 262176 | tf_op jit(solution)/shard_map/all_to_all | solution.py:13
  142.4 10.0 %collective-permute-start.5 = (f32[64,4,256]{2,0,1:T(8,128)S(1)}, f32[64,4,256]{2,0,1:T(8,128)}, u32[]{:S(2)}, u32[]{:S(2)}) collective-permute-start(f32[64,4,256]{2,0,1:T(8,128)S(1)} %slice.692), channel_id=1, source_target_pairs={{0,16},{4,20},{8,24},{12,28},{16,32},{20,36},{24,40},{28,44},{32,4... | collective-permute-start | bytes 786440 | tf_op jit(solution)/shard_map/ppermute | solution.py:25
  156.5 6.9 %collective-permute-done.6 = f32[64,4,256]{2,0,1:T(8,128)} collective-permute-done((f32[64,4,256]{2,0,1:T(8,128)S(1)}, f32[64,4,256]{2,0,1:T(8,128)}, u32[]{:S(2)}, u32[]{:S(2)}) %collective-permute-start.6) | collective-permute-done | bytes 262176 | tf_op jit(solution)/shard_map/ppermute | solution.py:25
  165.2 4.1 all-to-all-start.3
  169.3 6.7 %all-to-all-done.3 = f32[4,64,256]{2,1,0:T(8,128)} async-done(((f32[4,64,256]{2,1,0:T(8,128)}), f32[4,64,256]{2,1,0:T(8,128)}, u32[]{:S(2)}, u32[]{:S(2)}) %all-to-all-start.3) | async-done | bytes 262176 | tf_op jit(solution)/shard_map/all_to_all | solution.py:13
  177.9 6.0 %collective-permute-start.7 = (f32[64,3,256]{2,0,1:T(8,128)S(1)}, f32[64,3,256]{2,0,1:T(8,128)S(1)}, u32[]{:S(2)}, u32[]{:S(2)}) collective-permute-start(f32[64,3,256]{2,0,1:T(8,128)S(1)} %slice.695), channel_id=1, source_target_pairs={{0,32},{4,36},{8,40},{12,44},{16,48},{20,52},{24,56},{28,60},{32,6... | collective-permute-start | bytes 589832 | tf_op jit(solution)/shard_map/ppermute | solution.py:25
  187.1 15.5 %collective-permute-done.8 = f32[64,3,256]{2,0,1:T(8,128)S(1)} collective-permute-done((f32[64,3,256]{2,0,1:T(8,128)S(1)}, f32[64,3,256]{2,0,1:T(8,128)S(1)}, u32[]{:S(2)}, u32[]{:S(2)}) %collective-permute-start.8) | collective-permute-done | bytes 196640 | tf_op jit(solution)/shard_map/ppermute | solution.py:25
  203.4 4.1 all-to-all-start.4
  207.5 6.7 %all-to-all-done.4 = f32[4,64,256]{2,1,0:T(8,128)} async-done(((f32[4,64,256]{2,1,0:T(8,128)}), f32[4,64,256]{2,1,0:T(8,128)}, u32[]{:S(2)}, u32[]{:S(2)}) %all-to-all-start.4) | async-done | bytes 262176 | tf_op jit(solution)/shard_map/all_to_all | solution.py:13
  217.5 5.2 %collective-permute-start.9 = (f32[64,2,256]{2,0,1:T(8,128)S(1)}, f32[64,2,256]{2,0,1:T(8,128)}, u32[]{:S(2)}, u32[]{:S(2)}) collective-permute-start(f32[64,2,256]{2,0,1:T(8,128)S(1)} %slice.698), channel_id=1, source_target_pairs={{0,64},{4,68},{8,72},{12,76},{16,80},{20,84},{24,88},{28,92},{32,9... | collective-permute-start | bytes 393224 | tf_op jit(solution)/shard_map/ppermute | solution.py:25
  225.5 9.1 %all_to_all.122 = f32[4,64,256]{2,1,0:T(8,128)S(1)} all-to-all(f32[4,64,256]{2,1,0:T(8,128)S(1)} %tile.47), channel_id=1, replica_groups=mesh['leaf'=128,'sep'=4] {'sep'}, dimensions={0} | all-to-all | bytes 524288 | tf_op jit(solution)/shard_map/all_to_all | solution.py:13
  235.5 9.3 %collective-permute-start.11 = (f32[64,1,256]{2,0,1:T(8,128)S(1)}, f32[64,1,256]{2,0,1:T(8,128)S(1)}, u32[]{:S(2)}, u32[]{:S(2)}) collective-permute-start(f32[64,1,256]{2,0,1:T(8,128)S(1)} %slice_add_fusion), channel_id=1, source_target_pairs={{0,128},{4,132},{8,136},{12,140},{16,144},{20,148},{24,152},{28,15... | collective-permute-start | bytes 196616 | tf_op jit(solution)/shard_map/ppermute | solution.py:25
  246.7 8.7 %collective-permute-done.12 = f32[64,1,256]{2,0,1:T(8,128)S(1)} collective-permute-done((f32[64,1,256]{2,0,1:T(8,128)S(1)}, f32[64,1,256]{2,0,1:T(8,128)S(1)}, u32[]{:S(2)}, u32[]{:S(2)}) %collective-permute-start.12) | collective-permute-done | bytes 65568 | tf_op jit(solution)/shard_map/ppermute | solution.py:25
  255.5 9.1 %all_to_all.123 = f32[4,64,256]{2,1,0:T(8,128)S(1)} all-to-all(f32[4,64,256]{2,1,0:T(8,128)S(1)} %tile.48), channel_id=1, replica_groups=mesh['leaf'=128,'sep'=4] {'sep'}, dimensions={0} | all-to-all | bytes 524288 | tf_op jit(solution)/shard_map/all_to_all | solution.py:13
  265.8 6.0 %collective-permute-start.13 = (f32[64,1,256]{2,0,1:T(8,128)S(1)}, f32[64,1,256]{2,0,1:T(8,128)S(1)}, u32[]{:S(2)}, u32[]{:S(2)}) collective-permute-start(f32[64,1,256]{2,0,1:T(8,128)S(1)} %select_bitcast_fusion), channel_id=1, source_target_pairs={{0,128},{4,132},{8,136},{12,140},{16,144},{20,148},{24,152},{28,15... | collective-permute-start | bytes 196616 | tf_op jit(solution)/shard_map/ppermute | solution.py:25
  273.7 5.2 %collective-permute-done.14 = f32[64,1,256]{2,0,1:T(8,128)S(1)} collective-permute-done((f32[64,1,256]{2,0,1:T(8,128)S(1)}, f32[64,1,256]{2,0,1:T(8,128)S(1)}, u32[]{:S(2)}, u32[]{:S(2)}) %collective-permute-start.14) | collective-permute-done | bytes 65568 | tf_op jit(solution)/shard_map/ppermute | solution.py:25
  278.9 9.1 %all_to_all.124 = f32[4,64,256]{2,1,0:T(8,128)S(1)} all-to-all(f32[4,64,256]{2,1,0:T(8,128)S(1)} %tile.50), channel_id=1, replica_groups=mesh['leaf'=128,'sep'=4] {'sep'}, dimensions={0} | all-to-all | bytes 524288 | tf_op jit(solution)/shard_map/all_to_all | solution.py:13
  293.8 4.6 collective-permute-done.16
  298.5 9.1 %all_to_all.125 = f32[4,64,256]{2,1,0:T(8,128)S(1)} all-to-all(f32[4,64,256]{2,1,0:T(8,128)S(1)} %tile.52), channel_id=1, replica_groups=mesh['leaf'=128,'sep'=4] {'sep'}, dimensions={0} | all-to-all | bytes 524288 | tf_op jit(solution)/shard_map/all_to_all | solution.py:13
  309.4 5.1 %collective-permute-start.17 = (f32[64,3,256]{2,0,1:T(8,128)S(1)}, f32[64,3,256]{2,0,1:T(8,128)S(1)}, u32[]{:S(2)}, u32[]{:S(2)}) collective-permute-start(f32[64,3,256]{2,0,1:T(8,128)S(1)} %slice.705), channel_id=1, source_target_pairs={{0,32},{4,36},{8,40},{12,44},{16,48},{20,52},{24,56},{28,60},{32,6... | collective-permute-start | bytes 589832 | tf_op jit(solution)/shard_map/ppermute | solution.py:25
  315.8 3.2 collective-permute-done.17
  319.0 9.0 %collective-permute-done.18 = f32[64,3,256]{2,0,1:T(8,128)S(1)} collective-permute-done((f32[64,3,256]{2,0,1:T(8,128)S(1)}, f32[64,3,256]{2,0,1:T(8,128)S(1)}, u32[]{:S(2)}, u32[]{:S(2)}) %collective-permute-start.18) | collective-permute-done | bytes 196640 | tf_op jit(solution)/shard_map/ppermute | solution.py:25
  328.2 9.1 %all_to_all.126 = f32[4,64,256]{2,1,0:T(8,128)S(1)} all-to-all(f32[4,64,256]{2,1,0:T(8,128)S(1)} %tile.54), channel_id=1, replica_groups=mesh['leaf'=128,'sep'=4] {'sep'}, dimensions={0} | all-to-all | bytes 524288 | tf_op jit(solution)/shard_map/all_to_all | solution.py:13
  344.5 8.3 %collective-permute-done.20 = f32[64,4,256]{2,0,1:T(8,128)S(1)} collective-permute-done((f32[64,4,256]{2,0,1:T(8,128)S(1)}, f32[64,4,256]{2,0,1:T(8,128)S(1)}, u32[]{:S(2)}, u32[]{:S(2)}) %collective-permute-start.20) | collective-permute-done | bytes 262176 | tf_op jit(solution)/shard_map/ppermute | solution.py:25
  352.9 9.1 %all_to_all.127 = f32[4,64,256]{2,1,0:T(8,128)S(1)} all-to-all(f32[4,64,256]{2,1,0:T(8,128)S(1)} %tile.56), channel_id=1, replica_groups=mesh['leaf'=128,'sep'=4] {'sep'}, dimensions={0} | all-to-all | bytes 524288 | tf_op jit(solution)/shard_map/all_to_all | solution.py:13
  363.9 7.7 %collective-permute-start.21 = (f32[64,5,256]{2,0,1:T(8,128)S(1)}, f32[64,5,256]{2,0,1:T(8,128)S(1)}, u32[]{:S(2)}, u32[]{:S(2)}) collective-permute-start(f32[64,5,256]{2,0,1:T(8,128)S(1)} %slice.711), channel_id=1, source_target_pairs={{0,8},{4,12},{8,16},{12,20},{16,24},{20,28},{24,32},{28,36},{32,40... | collective-permute-start | bytes 983048 | tf_op jit(solution)/shard_map/ppermute | solution.py:25
  376.1 5.5 %collective-permute-done.22 = f32[64,5,256]{2,0,1:T(8,128)S(1)} collective-permute-done((f32[64,5,256]{2,0,1:T(8,128)S(1)}, f32[64,5,256]{2,0,1:T(8,128)S(1)}, u32[]{:S(2)}, u32[]{:S(2)}) %collective-permute-start.22) | collective-permute-done | bytes 327712 | tf_op jit(solution)/shard_map/ppermute | solution.py:25
  381.9 9.1 %all_to_all.128 = f32[4,64,256]{2,1,0:T(8,128)S(1)} all-to-all(f32[4,64,256]{2,1,0:T(8,128)S(1)} %tile.58), channel_id=1, replica_groups=mesh['leaf'=128,'sep'=4] {'sep'}, dimensions={0} | all-to-all | bytes 524288 | tf_op jit(solution)/shard_map/all_to_all | solution.py:13
  394.7 3.6 collective-permute-start.24
  398.4 3.5 collective-permute-done.23
  403.9 9.1 %all_to_all.129 = f32[4,64,256]{2,1,0:T(8,128)S(1)} all-to-all(f32[4,64,256]{2,1,0:T(8,128)S(1)} %tile.60), channel_id=1, replica_groups=mesh['leaf'=128,'sep'=4] {'sep'}, dimensions={0} | all-to-all | bytes 524288 | tf_op jit(solution)/shard_map/all_to_all | solution.py:13
  417.5 6.0 %collective-permute-done.25 = f32[64,7,256]{2,0,1:T(8,128)S(1)} collective-permute-done((f32[64,7,256]{2,0,1:T(8,128)S(1)}, f32[64,7,256]{2,0,1:T(8,128)S(1)}, u32[]{:S(2)}, u32[]{:S(2)}) %collective-permute-start.25) | collective-permute-done | bytes 458784 | tf_op jit(solution)/shard_map/ppermute | solution.py:25
  425.3 3.7 all-to-all-start.13
  429.2 26.0 %all-to-all-done.13 = f32[256,7,256]{2,1,0:T(8,128)S(1)} async-done(((f32[256,7,256]{2,1,0:T(8,128)}), f32[256,7,256]{2,1,0:T(8,128)S(1)}, u32[]{:S(2)}, u32[]{:S(2)}) %all-to-all-start.13) | async-done | bytes 1835040 | tf_op jit(solution)/shard_map/all_to_all | solution.py:13
  460.9 21.8 %reduce-scatter.7.cloned.1.call-done = f32[160,256]{1,0:T(8,128)} async-done(((f32[640,256]{1,0:T(8,128)}), f32[160,256]{1,0:T(8,128)}) %reduce-scatter.7.cloned.1.call-update) | async-done | bytes 163856
  (170 shorter events, 89.7 us)
Async XLA Ops:
  7.2 16.1 %copy-start = (f32[1,896,160]{1,2,0:T(8,128)S(1)}, f32[1,896,160]{1,2,0:T(8,128)}, u32[]{:S(2)}) copy-start(f32[1,896,160]{1,2,0:T(8,128)} %param.64) | copy-start | bytes 1720324
  7.2 60.4 %reduce-scatter.5.cloned.1.call-start = ((), (), s32[]{:S(2)}) async-start(), calls=%async_computation.16 | async-start | bytes 2621440 | tf_op jit(solution)/shard_map/reduce_scatter | solution.py:86
  21.7 3.0 copy-start.11
  27.7 52.0 %copy-start.3 = (f32[1,64,256]{2,1,0:T(8,128)S(1)}, f32[1,64,256]{2,1,0:T(8,128)}, u32[]{:S(2)}) copy-start(f32[1,64,256]{2,1,0:T(8,128)} %param.67) | copy-start | bytes 196612
  27.8 62.8 %copy-start.1 = (f32[1,256,256]{2,1,0:T(8,128)S(1)}, f32[1,256,256]{2,1,0:T(8,128)}, u32[]{:S(2)}) copy-start(f32[1,256,256]{2,1,0:T(8,128)} %param.68) | copy-start | bytes 786436
  27.8 63.4 %copy-start.2 = (f32[1,256,256]{2,1,0:T(8,128)S(1)}, f32[1,256,256]{2,1,0:T(8,128)}, u32[]{:S(2)}) copy-start(f32[1,256,256]{2,1,0:T(8,128)} %param.69) | copy-start | bytes 786436
  68.8 9.8 %collective-permute-start = (f32[64,7,256]{2,0,1:T(8,128)S(1)}, f32[64,7,256]{2,0,1:T(8,128)S(1)}, u32[]{:S(2)}, u32[]{:S(2)}) collective-permute-start(f32[64,7,256]{2,0,1:T(8,128)S(1)} %copy.93), channel_id=1, source_target_pairs={{0,4},{4,8},{8,12},{12,16},{16,20},{20,24},{24,28},{28,32},{32,36}... | collective-permute-start | bytes 1376264 | tf_op jit(solution)/shard_map/ppermute | solution.py:25
  80.5 10.1 %all-to-all-start = ((f32[4,64,256]{2,1,0:T(8,128)}), f32[4,64,256]{2,1,0:T(8,128)S(1)}, u32[]{:S(2)}, u32[]{:S(2)}) async-start(f32[4,64,256]{2,1,0:T(8,128)} %tile.42), calls=%async_computation.1 | async-start | bytes 524288 | tf_op jit(solution)/shard_map/all_to_all | solution.py:13
  91.6 9.1 %collective-permute-start.1 = (f32[64,6,256]{2,0,1:T(8,128)S(1)}, f32[64,6,256]{2,0,1:T(8,128)S(1)}, u32[]{:S(2)}, u32[]{:S(2)}) collective-permute-start(f32[64,6,256]{2,0,1:T(8,128)S(1)} %slice.686), channel_id=1, source_target_pairs={{0,4},{4,8},{8,12},{12,16},{16,20},{20,24},{24,28},{28,32},{32,36}... | collective-permute-start | bytes 1179656 | tf_op jit(solution)/shard_map/ppermute | solution.py:25
  93.6 8.9 %collective-permute-start.2 = (f32[64,6,256]{2,0,1:T(8,128)S(1)}, f32[64,6,256]{2,0,1:T(8,128)}, u32[]{:S(2)}, u32[]{:S(2)}) collective-permute-start(f32[64,6,256]{2,0,1:T(8,128)S(1)} %slice.686), channel_id=1, source_target_pairs={{4,0},{8,4},{12,8},{16,12},{20,16},{24,20},{28,24},{32,28},{36,32}... | collective-permute-start | bytes 1179656 | tf_op jit(solution)/shard_map/ppermute | solution.py:25
  104.3 10.6 %all-to-all-start.1 = ((f32[4,64,256]{2,1,0:T(8,128)}), f32[4,64,256]{2,1,0:T(8,128)S(1)}, u32[]{:S(2)}, u32[]{:S(2)}) async-start(f32[4,64,256]{2,1,0:T(8,128)} %tile.43), calls=%async_computation.2 | async-start | bytes 524288 | tf_op jit(solution)/shard_map/all_to_all | solution.py:13
  115.9 12.2 %collective-permute-start.3 = (f32[64,5,256]{2,0,1:T(8,128)S(1)}, f32[64,5,256]{2,0,1:T(8,128)S(1)}, u32[]{:S(2)}, u32[]{:S(2)}) collective-permute-start(f32[64,5,256]{2,0,1:T(8,128)S(1)} %slice.689), channel_id=1, source_target_pairs={{0,8},{4,12},{8,16},{12,20},{16,24},{20,28},{24,32},{28,36},{32,40... | collective-permute-start | bytes 983048 | tf_op jit(solution)/shard_map/ppermute | solution.py:25
  118.8 10.5 %collective-permute-start.4 = (f32[64,5,256]{2,0,1:T(8,128)S(1)}, f32[64,5,256]{2,0,1:T(8,128)}, u32[]{:S(2)}, u32[]{:S(2)}) collective-permute-start(f32[64,5,256]{2,0,1:T(8,128)S(1)} %slice.689), channel_id=1, source_target_pairs={{8,0},{12,4},{16,8},{20,12},{24,16},{28,20},{32,24},{36,28},{40,32... | collective-permute-start | bytes 983048 | tf_op jit(solution)/shard_map/ppermute | solution.py:25
  131.1 10.3 %all-to-all-start.2 = ((f32[4,64,256]{2,1,0:T(8,128)}), f32[4,64,256]{2,1,0:T(8,128)S(1)}, u32[]{:S(2)}, u32[]{:S(2)}) async-start(f32[4,64,256]{2,1,0:T(8,128)} %tile.44), calls=%async_computation.3 | async-start | bytes 524288 | tf_op jit(solution)/shard_map/all_to_all | solution.py:13
  142.4 14.0 %collective-permute-start.5 = (f32[64,4,256]{2,0,1:T(8,128)S(1)}, f32[64,4,256]{2,0,1:T(8,128)}, u32[]{:S(2)}, u32[]{:S(2)}) collective-permute-start(f32[64,4,256]{2,0,1:T(8,128)S(1)} %slice.692), channel_id=1, source_target_pairs={{0,16},{4,20},{8,24},{12,28},{16,32},{20,36},{24,40},{28,44},{32,4... | collective-permute-start | bytes 786440 | tf_op jit(solution)/shard_map/ppermute | solution.py:25
  152.4 11.0 %collective-permute-start.6 = (f32[64,4,256]{2,0,1:T(8,128)S(1)}, f32[64,4,256]{2,0,1:T(8,128)}, u32[]{:S(2)}, u32[]{:S(2)}) collective-permute-start(f32[64,4,256]{2,0,1:T(8,128)S(1)} %slice.692), channel_id=1, source_target_pairs={{16,0},{20,4},{24,8},{28,12},{32,16},{36,20},{40,24},{44,28},{48,3... | collective-permute-start | bytes 786440 | tf_op jit(solution)/shard_map/ppermute | solution.py:25
  165.2 10.8 %all-to-all-start.3 = ((f32[4,64,256]{2,1,0:T(8,128)}), f32[4,64,256]{2,1,0:T(8,128)}, u32[]{:S(2)}, u32[]{:S(2)}) async-start(f32[4,64,256]{2,1,0:T(8,128)} %tile.45), calls=%async_computation.4 | async-start | bytes 524288 | tf_op jit(solution)/shard_map/all_to_all | solution.py:13
  177.9 9.2 %collective-permute-start.7 = (f32[64,3,256]{2,0,1:T(8,128)S(1)}, f32[64,3,256]{2,0,1:T(8,128)S(1)}, u32[]{:S(2)}, u32[]{:S(2)}) collective-permute-start(f32[64,3,256]{2,0,1:T(8,128)S(1)} %slice.695), channel_id=1, source_target_pairs={{0,32},{4,36},{8,40},{12,44},{16,48},{20,52},{24,56},{28,60},{32,6... | collective-permute-start | bytes 589832 | tf_op jit(solution)/shard_map/ppermute | solution.py:25
  184.0 18.6 %collective-permute-start.8 = (f32[64,3,256]{2,0,1:T(8,128)S(1)}, f32[64,3,256]{2,0,1:T(8,128)S(1)}, u32[]{:S(2)}, u32[]{:S(2)}) collective-permute-start(f32[64,3,256]{2,0,1:T(8,128)S(1)} %slice.695), channel_id=1, source_target_pairs={{32,0},{36,4},{40,8},{44,12},{48,16},{52,20},{56,24},{60,28},{64,3... | collective-permute-start | bytes 589832 | tf_op jit(solution)/shard_map/ppermute | solution.py:25
  203.4 10.8 %all-to-all-start.4 = ((f32[4,64,256]{2,1,0:T(8,128)}), f32[4,64,256]{2,1,0:T(8,128)}, u32[]{:S(2)}, u32[]{:S(2)}) async-start(f32[4,64,256]{2,1,0:T(8,128)} %tile.46), calls=%async_computation.5 | async-start | bytes 524288 | tf_op jit(solution)/shard_map/all_to_all | solution.py:13
  216.2 6.9 %collective-permute-start.10 = (f32[64,2,256]{2,0,1:T(8,128)S(1)}, f32[64,2,256]{2,0,1:T(8,128)S(1)}, u32[]{:S(2)}, u32[]{:S(2)}) collective-permute-start(f32[64,2,256]{2,0,1:T(8,128)S(1)} %slice.698), channel_id=1, source_target_pairs={{64,0},{68,4},{72,8},{76,12},{80,16},{84,20},{88,24},{92,28},{96,3... | collective-permute-start | bytes 393224 | tf_op jit(solution)/shard_map/ppermute | solution.py:25
  217.5 7.1 %collective-permute-start.9 = (f32[64,2,256]{2,0,1:T(8,128)S(1)}, f32[64,2,256]{2,0,1:T(8,128)}, u32[]{:S(2)}, u32[]{:S(2)}) collective-permute-start(f32[64,2,256]{2,0,1:T(8,128)S(1)} %slice.698), channel_id=1, source_target_pairs={{0,64},{4,68},{8,72},{12,76},{16,80},{20,84},{24,88},{28,92},{32,9... | collective-permute-start | bytes 393224 | tf_op jit(solution)/shard_map/ppermute | solution.py:25
  235.5 11.2 %collective-permute-start.11 = (f32[64,1,256]{2,0,1:T(8,128)S(1)}, f32[64,1,256]{2,0,1:T(8,128)S(1)}, u32[]{:S(2)}, u32[]{:S(2)}) collective-permute-start(f32[64,1,256]{2,0,1:T(8,128)S(1)} %slice_add_fusion), channel_id=1, source_target_pairs={{0,128},{4,132},{8,136},{12,140},{16,144},{20,148},{24,152},{28,15... | collective-permute-start | bytes 196616 | tf_op jit(solution)/shard_map/ppermute | solution.py:25
  244.9 10.6 %collective-permute-start.12 = (f32[64,1,256]{2,0,1:T(8,128)S(1)}, f32[64,1,256]{2,0,1:T(8,128)S(1)}, u32[]{:S(2)}, u32[]{:S(2)}) collective-permute-start(f32[64,1,256]{2,0,1:T(8,128)S(1)} %slice_add_fusion), channel_id=1, source_target_pairs={{128,0},{132,4},{136,8},{140,12},{144,16},{148,20},{152,24},{156,2... | collective-permute-start | bytes 196616 | tf_op jit(solution)/shard_map/ppermute | solution.py:25
  265.8 7.9 %collective-permute-start.13 = (f32[64,1,256]{2,0,1:T(8,128)S(1)}, f32[64,1,256]{2,0,1:T(8,128)S(1)}, u32[]{:S(2)}, u32[]{:S(2)}) collective-permute-start(f32[64,1,256]{2,0,1:T(8,128)S(1)} %select_bitcast_fusion), channel_id=1, source_target_pairs={{0,128},{4,132},{8,136},{12,140},{16,144},{20,148},{24,152},{28,15... | collective-permute-start | bytes 196616 | tf_op jit(solution)/shard_map/ppermute | solution.py:25
  271.8 7.1 %collective-permute-start.14 = (f32[64,1,256]{2,0,1:T(8,128)S(1)}, f32[64,1,256]{2,0,1:T(8,128)S(1)}, u32[]{:S(2)}, u32[]{:S(2)}) collective-permute-start(f32[64,1,256]{2,0,1:T(8,128)S(1)} %select_bitcast_fusion), channel_id=1, source_target_pairs={{128,0},{132,4},{136,8},{140,12},{144,16},{148,20},{152,24},{156,2... | collective-permute-start | bytes 196616 | tf_op jit(solution)/shard_map/ppermute | solution.py:25
  289.8 3.9 collective-permute-start.15
  291.3 7.1 %collective-permute-start.16 = (f32[64,2,256]{2,0,1:T(8,128)S(1)}, f32[64,2,256]{2,0,1:T(8,128)S(1)}, u32[]{:S(2)}, u32[]{:S(2)}) collective-permute-start(f32[64,2,256]{2,0,1:T(8,128)S(1)} %slice.702), channel_id=1, source_target_pairs={{64,0},{68,4},{72,8},{76,12},{80,16},{84,20},{88,24},{92,28},{96,3... | collective-permute-start | bytes 393224 | tf_op jit(solution)/shard_map/ppermute | solution.py:25
  309.4 9.6 %collective-permute-start.17 = (f32[64,3,256]{2,0,1:T(8,128)S(1)}, f32[64,3,256]{2,0,1:T(8,128)S(1)}, u32[]{:S(2)}, u32[]{:S(2)}) collective-permute-start(f32[64,3,256]{2,0,1:T(8,128)S(1)} %slice.705), channel_id=1, source_target_pairs={{0,32},{4,36},{8,40},{12,44},{16,48},{20,52},{24,56},{28,60},{32,6... | collective-permute-start | bytes 589832 | tf_op jit(solution)/shard_map/ppermute | solution.py:25
  314.5 13.6 %collective-permute-start.18 = (f32[64,3,256]{2,0,1:T(8,128)S(1)}, f32[64,3,256]{2,0,1:T(8,128)S(1)}, u32[]{:S(2)}, u32[]{:S(2)}) collective-permute-start(f32[64,3,256]{2,0,1:T(8,128)S(1)} %slice.705), channel_id=1, source_target_pairs={{32,0},{36,4},{40,8},{44,12},{48,16},{52,20},{56,24},{60,28},{64,3... | collective-permute-start | bytes 589832 | tf_op jit(solution)/shard_map/ppermute | solution.py:25
  339.1 5.4 %collective-permute-start.19 = (f32[64,4,256]{2,0,1:T(8,128)S(1)}, f32[64,4,256]{2,0,1:T(8,128)S(1)}, u32[]{:S(2)}, u32[]{:S(2)}) collective-permute-start(f32[64,4,256]{2,0,1:T(8,128)S(1)} %slice.708), channel_id=1, source_target_pairs={{0,16},{4,20},{8,24},{12,28},{16,32},{20,36},{24,40},{28,44},{32,4... | collective-permute-start | bytes 786440 | tf_op jit(solution)/shard_map/ppermute | solution.py:25
  340.6 12.1 %collective-permute-start.20 = (f32[64,4,256]{2,0,1:T(8,128)S(1)}, f32[64,4,256]{2,0,1:T(8,128)S(1)}, u32[]{:S(2)}, u32[]{:S(2)}) collective-permute-start(f32[64,4,256]{2,0,1:T(8,128)S(1)} %slice.708), channel_id=1, source_target_pairs={{16,0},{20,4},{24,8},{28,12},{32,16},{36,20},{40,24},{44,28},{48,3... | collective-permute-start | bytes 786440 | tf_op jit(solution)/shard_map/ppermute | solution.py:25
  363.9 12.2 %collective-permute-start.21 = (f32[64,5,256]{2,0,1:T(8,128)S(1)}, f32[64,5,256]{2,0,1:T(8,128)S(1)}, u32[]{:S(2)}, u32[]{:S(2)}) collective-permute-start(f32[64,5,256]{2,0,1:T(8,128)S(1)} %slice.711), channel_id=1, source_target_pairs={{0,8},{4,12},{8,16},{12,20},{16,24},{20,28},{24,32},{28,36},{32,40... | collective-permute-start | bytes 983048 | tf_op jit(solution)/shard_map/ppermute | solution.py:25
  371.6 10.1 %collective-permute-start.22 = (f32[64,5,256]{2,0,1:T(8,128)S(1)}, f32[64,5,256]{2,0,1:T(8,128)S(1)}, u32[]{:S(2)}, u32[]{:S(2)}) collective-permute-start(f32[64,5,256]{2,0,1:T(8,128)S(1)} %slice.711), channel_id=1, source_target_pairs={{8,0},{12,4},{16,8},{20,12},{24,16},{28,20},{32,24},{36,28},{40,32... | collective-permute-start | bytes 983048 | tf_op jit(solution)/shard_map/ppermute | solution.py:25
  392.8 9.1 %collective-permute-start.23 = (f32[64,6,256]{2,0,1:T(8,128)S(1)}, f32[64,6,256]{2,0,1:T(8,128)S(1)}, u32[]{:S(2)}, u32[]{:S(2)}) collective-permute-start(f32[64,6,256]{2,0,1:T(8,128)S(1)} %slice.714), channel_id=1, source_target_pairs={{0,4},{4,8},{8,12},{12,16},{16,20},{20,24},{24,28},{28,32},{32,36}... | collective-permute-start | bytes 1179656 | tf_op jit(solution)/shard_map/ppermute | solution.py:25
  394.7 8.9 %collective-permute-start.24 = (f32[64,6,256]{2,0,1:T(8,128)S(1)}, f32[64,6,256]{2,0,1:T(8,128)S(1)}, u32[]{:S(2)}, u32[]{:S(2)}) collective-permute-start(f32[64,6,256]{2,0,1:T(8,128)S(1)} %slice.714), channel_id=1, source_target_pairs={{4,0},{8,4},{12,8},{16,12},{20,16},{24,20},{28,24},{32,28},{36,32}... | collective-permute-start | bytes 1179656 | tf_op jit(solution)/shard_map/ppermute | solution.py:25
  414.9 8.6 %collective-permute-start.25 = (f32[64,7,256]{2,0,1:T(8,128)S(1)}, f32[64,7,256]{2,0,1:T(8,128)S(1)}, u32[]{:S(2)}, u32[]{:S(2)}) collective-permute-start(f32[64,7,256]{2,0,1:T(8,128)S(1)} %get-tuple-element.328), channel_id=1, source_target_pairs={{4,0},{8,4},{12,8},{16,12},{20,16},{24,20},{28,24},{32,28},{36,32}... | collective-permute-start | bytes 1376264 | tf_op jit(solution)/shard_map/ppermute | solution.py:25
  425.3 3.8 copy-start.12
  425.3 29.9 %all-to-all-start.13 = ((f32[256,7,256]{2,1,0:T(8,128)}), f32[256,7,256]{2,1,0:T(8,128)S(1)}, u32[]{:S(2)}, u32[]{:S(2)}) async-start(f32[256,7,256]{2,1,0:T(8,128)} %bitcast.65), calls=%async_computation.14 | async-start | bytes 4194304 | tf_op jit(solution)/shard_map/all_to_all | solution.py:13
  429.1 53.6 %reduce-scatter.7.cloned.1.call-start = ((), (), s32[]{:S(2)}) async-start(), calls=%async_computation.17 | async-start | bytes 819200
  429.2 28.1 %copy-start.4 = (f32[1,160,640]{2,1,0:T(8,128)S(1)}, f32[1,160,640]{2,1,0:T(8,128)}, u32[]{:S(2)}) copy-start(f32[1,160,640]{2,1,0:T(8,128)} %param.63) | copy-start | bytes 1228804
  457.3 2.2 copy-start.5
  457.3 2.3 copy-start.6
  457.3 2.4 copy-start.7
  458.2 1.6 copy-start.8
  458.2 1.7 copy-start.9
  458.2 1.8 copy-start.10
Sparse Core Ops, SparseCore 0:
  27.9 39.6 reduce-scatter.4
  459.4 23.2 reduce-scatter.6
